TPU v7x, 32 devices: a whole 2x2x4 slice. The times are simulated.
32 devices in a mesh: rep: 8 (over z, core), rows: 4 (over y, x).
Axes of the slice: x: 2, y: 2, z: 4, core: 2. Of those that a mesh axis runs over, the one named last changes fastest.
Arguments:
- weights: bfloat16 [7168, 2048], P('rows'), may hold values from -6 to 6
- momentum: float32 [8, 7168, 2048], P('rep', 'rows'), may hold values from -8 to 8
- gradient: bfloat16 [8, 7168, 2048], P('rep', 'rows'), may hold values from -8 to 8
- right_factor: float32 [2048, 512], P('rows'), may hold values from -6 to 6
Outputs:
- new_weights: bfloat16 [7168, 2048], P('rows')
- new_momentum: float32 [8, 7168, 2048], P('rep', 'rows')
- new_right: float32 [2048, 512], P('rows')
All inputs are finite; a program needn't handle non-finite values.
Results may differ from a plain program's by a relative error of at most 0.019.
Values may be sent and summed in bfloat16 or wider, within the bound.
A program may use at most 128 MiB of HBM per device.

v0:
```python
import jax
import jax.numpy as jnp
from jax import lax
from jax.sharding import PartitionSpec as P

M = 7168
N = 2048
momentum_keep = 0.05
learn_rate = 0.5
tiny = 1e-06


def per_device(weights, momentum, gradient, right_factor):
    groups = lax.axis_size("rep")
    shards = lax.axis_size("rows")
    combined = momentum[0] + gradient[0].astype(jnp.float32)
    combined_half = combined.astype(jnp.bfloat16)
    columns = combined.shape[1]
    share = columns // shards
    left_local = jnp.dot(
        combined_half,
        lax.all_gather(right_factor.astype(jnp.bfloat16), "rows", axis=0, tiled=True),
        preferred_element_type=jnp.float32,
    )
    left_local = lax.optimization_barrier(left_local.astype(jnp.bfloat16)).astype(jnp.float32)
    left_mean = lax.psum(left_local.astype(jnp.bfloat16), "rep").astype(jnp.float32) / groups
    gram = lax.psum(jnp.dot(left_mean.T, left_mean, precision=lax.Precision.HIGHEST), "rows")
    chol = jnp.linalg.cholesky(gram)
    left_orth = jax.scipy.linalg.solve_triangular(chol, left_mean.T, lower=True).T
    left_half = left_orth.astype(jnp.bfloat16)
    partial_right = jnp.einsum(
        "ij,ik->jk", combined_half, left_half, preferred_element_type=jnp.float32
    )
    right_mean = lax.psum(partial_right, ("rep", "rows")) / groups
    normed = right_mean / jnp.sqrt(jnp.mean(right_mean * right_mean, axis=0) + tiny)
    feedback = jnp.dot(
        left_half, right_mean.astype(jnp.bfloat16).T, preferred_element_type=jnp.float32
    )
    update = jnp.dot(left_half, normed.astype(jnp.bfloat16).T, preferred_element_type=jnp.float32)
    new_right = lax.dynamic_slice_in_dim(normed, lax.axis_index("rows") * share, share, 0)
    new_momentum = combined - momentum_keep * feedback
    new_weights = (weights.astype(jnp.float32) - learn_rate * jnp.sqrt(M / N) * update).astype(
        jnp.bfloat16
    )
    return (new_weights, new_momentum[None], new_right)


def solution(mesh):
    in_specs = (P("rows", None), P("rep", "rows", None), P("rep", "rows", None), P("rows", None))
    out_specs = (P("rows", None), P("rep", "rows", None), P("rows", None))
    return jax.shard_map(
        per_device, mesh=mesh, in_specs=in_specs, out_specs=out_specs, check_vma=False
    )
```

profile of v0, /device:TPU:0, one launch (start us, length us, event | category | flops | bytes accessed | tf_op | source)
XLA Modules:
  0.0 525.9 jit_solution(10342217912073874617)
XLA Ops:
  9.4 39.0 %all-gather.2.cloned.1.call-done = bf16[2048,512]{1,0:T(8,128)(2,1)} async-done(((bf16[512,512]{1,0:T(8,128)(2,1)}), bf16[2048,512]{1,0:T(8,128)(2,1)}) %all-gather.2.cloned.1.call-update) | async-done | bytes 2097168 | tf_op jit(solution)/shard_map/all_gather | solution.py:22
  48.3 13.1 %convolution_convert_fusion = bf16[1792,512]{1,0:T(8,128)(2,1)} fusion(bf16[2048,512]{1,0:T(8,128)(2,1)} %all-gather.2.cloned.1.call-done, f32[1,1792,2048]{2,1,0:T(8,128)} %param.5, bf16[1,1792,2048]{2,1,0:T(8,128)(2,1)} %param.6), kind=kOutput, calls=%fused_computation.13 | convolution fusion | flops 3770023936 | bytes 25952256 | tf_op jit(solution)/shard_map/dot_general | solution.py:20
  61.5 63.3 %all-reduce.5.cloned.1.call-done = bf16[1792,512]{1,0:T(8,128)(2,1)} async-done(((bf16[1792,512]{1,0:T(8,128)(2,1)}), bf16[1792,512]{1,0:T(8,128)(2,1)}) %all-reduce.5.cloned.1.call-update) | async-done | bytes 1835024 | tf_op jit(solution)/shard_map/psum | solution.py:26
  124.7 9.4 %fusion.2 = f32[512,512]{0,1:T(8,128)} fusion(bf16[1792,512]{1,0:T(8,128)(2,1)} %all-reduce.5.cloned.1.call-done), kind=kOutput, calls=%fused_computation.12 | convolution fusion | flops 5638979584 | bytes 2883584 | tf_op jit(solution)/shard_map/dot_general | solution.py:27
  134.4 2.4 fusion.1
  136.8 50.0 %all-reduce.7.cloned.1.call-done = f32[512,512]{0,1:T(8,128)} async-done(((f32[512,512]{0,1:T(8,128)}), f32[512,512]{0,1:T(8,128)}) %all-reduce.7.cloned.1.call-update) | async-done | bytes 1048592 | tf_op jit(solution)/shard_map/psum | solution.py:27
  189.8 11.7 %cholesky.104 = f32[128,128]{1,0:T(8,128)S(1)} custom-call(f32[128,128]{1,0:T(8,128)S(1)} %cholesky.266), custom_call_target="Cholesky" | custom-call | tf_op jit(solution)/shard_map/jit(cholesky)/cholesky | solution.py:28
  201.5 9.8 %custom-call.31 = f32[1,128,128]{1,2,0:T(8,128)S(1)} custom-call(f32[1,128,128]{2,1,0:T(8,128)S(1)} %get-tuple-element.30), custom_call_target="InvertDiagBlocksLowerTriangular" | custom-call | tf_op jit(solution)/shard_map/jit(cholesky)/cholesky | solution.py:28
  212.2 11.7 %cholesky.217 = f32[128,128]{1,0:T(8,128)S(1)} custom-call(f32[128,128]{1,0:T(8,128)S(1)} %cholesky.270), custom_call_target="Cholesky" | custom-call | tf_op jit(solution)/shard_map/jit(cholesky)/cholesky | solution.py:28
  223.9 10.2 %custom-call.32 = f32[1,128,128]{1,2,0:T(8,128)S(1)} custom-call(f32[1,128,128]{2,1,0:T(8,128)S(1)} %get-tuple-element.27), custom_call_target="InvertDiagBlocksLowerTriangular" | custom-call | tf_op jit(solution)/shard_map/jit(cholesky)/cholesky | solution.py:28
  234.8 11.7 %cholesky.238 = f32[128,128]{1,0:T(8,128)S(1)} custom-call(f32[128,128]{1,0:T(8,128)S(1)} %cholesky.275), custom_call_target="Cholesky" | custom-call | tf_op jit(solution)/shard_map/jit(cholesky)/cholesky | solution.py:28
  247.3 9.8 %custom-call.33 = f32[1,128,128]{1,2,0:T(8,128)S(1)} custom-call(f32[1,128,128]{2,1,0:T(8,128)S(1)} %get-tuple-element.24), custom_call_target="InvertDiagBlocksLowerTriangular" | custom-call | tf_op jit(solution)/shard_map/jit(cholesky)/cholesky | solution.py:28
  257.7 11.9 %cholesky.255 = f32[128,128]{1,0:T(8,128)S(1)} custom-call(f32[128,128]{1,0:T(8,128)S(1)} %convolution_subtract_fusion.4), custom_call_target="Cholesky" | custom-call | tf_op jit(solution)/shard_map/jit(cholesky)/cholesky | solution.py:28
  273.6 8.5 %while.1 = (s32[]{:T(128)}, f32[512,512]{1,0:T(8,128)S(1)}, s32[4,2]{0,1:T(2,128)S(1)}, f32[4,128,128]{2,1,0:T(8,128)S(1)}, s32[]{:T(128)}) while((s32[]{:T(128)}, f32[512,512]{1,0:T(8,128)S(1)}, s32[4,2]{0,1:T(2,128)S(1)}, f32[4,128,128]{2,1,0:T(8,128)S(1)}, s32[]{:T(128)}) %tuple.34), condition=%wide.while_cond, body=%wide.while_body.sunk | while | flops 2 | bytes 131181 | solution.py:29
  282.1 39.3 %custom-call.34 = f32[4,128,128]{1,2,0:T(8,128)S(1)} custom-call(f32[4,128,128]{2,1,0:T(8,128)S(1)} %get-tuple-element.10), custom_call_target="InvertDiagBlocksLowerTriangular" | custom-call | tf_op jit(solution)/shard_map/jit(_solve_triangular)/triangular_solve | solution.py:29
  321.4 2.3 fusion.45
  323.7 2.8 convolution_subtract_fusion.1
  327.5 3.2 convolution_subtract_fusion
  331.7 4.7 fusion.9
  338.3 11.3 %fusion.41 = f32[2048,512]{1,0:T(8,128)} fusion(f32[1,1792,2048]{2,1,0:T(8,128)} %param.5, bf16[1,1792,2048]{2,1,0:T(8,128)(2,1)S(1)} %bitcast.67, bf16[128,1792]{1,0:T(8,128)(2,1)S(1)} %convolution_convert_fusion.1, bf16[128,1792]{1,0:T(8,128)(2,1)S(1)} %get-tuple-element.33, bf16[128,1792]{1,0:T(8,128)(2,1)S(1)} %get-tuple-element.35, ...), kind=kOutput, calls=%fused_computation.86 | convolution fusion | flops 3776446464 | bytes 28049408 | tf_op jit(solution)/shard_map/ij,ik->jk/dot_general | solution.py:31
  349.6 142.5 %all-reduce.9.cloned.1.call-done = f32[2048,512]{1,0:T(8,128)} async-done(((f32[2048,512]{1,0:T(8,128)}), f32[2048,512]{1,0:T(8,128)}) %all-reduce.9.cloned.1.call-update) | async-done | bytes 4194320 | tf_op jit(solution)/shard_map/psum | solution.py:34
  492.1 2.9 multiply_reduce_fusion
  496.7 8.2 %subtract_convert_fusion = bf16[1792,2048]{1,0:T(8,128)(2,1)} fusion(bf16[1792,2048]{1,0:T(8,128)(2,1)} %param.4, f32[2048,512]{1,0:T(8,128)S(1)} %multiply_divide_fusion, bf16[128,1792]{1,0:T(8,128)(2,1)S(1)} %copy-done.6, bf16[128,1792]{1,0:T(8,128)(2,1)S(1)} %copy-done.4, bf16[128,1792]{1,0:T(8,128)(2,1)S(1)} %get-tuple-element.35, ...), kind=kOutput, calls=%fused_computation.5 | convolution fusion | flops 3781165056 | bytes 20709376 | tf_op jit(solution)/shard_map/dot_general | solution.py:39
  506.0 13.0 %fusion = f32[1,1792,2048]{2,1,0:T(8,128)} fusion(f32[1,1792,2048]{2,1,0:T(8,128)} %param.5, bf16[1,1792,2048]{2,1,0:T(8,128)(2,1)} %param.6, f32[2048,512]{1,0:T(8,128)S(1)} %copy-done, bf16[128,1792]{1,0:T(8,128)(2,1)} %copy-done.5, bf16[128,1792]{1,0:T(8,128)(2,1)} %copy-done.3, bf16[128,1792]{1,0:T(8,128)(2,1)S(1)} %get-tuple-element.35, ...), kind=kOutput, calls=%fused_computation.4 | convolution fusion | flops 3782213632 | bytes 42729472 | tf_op jit(solution)/shard_map/dot_general | solution.py:36
  (69 shorter events, 24.9 us)
Async XLA Ops:
  7.2 41.2 %all-gather.2.cloned.1.call-start = ((), (), s32[]{:S(2)}) async-start(), calls=%async_computation | async-start | bytes 2621440 | tf_op jit(solution)/shard_map/all_gather | solution.py:22
  9.3 115.4 %all-reduce.5.cloned.1.call-start = ((), (), s32[]{:S(2)}) async-start(), calls=%async_computation.1 | async-start | bytes 3670016 | tf_op jit(solution)/shard_map/psum | solution.py:26
  61.4 125.4 %all-reduce.7.cloned.1.call-start = ((), (), s32[]{:S(2)}) async-start(), calls=%async_computation.2 | async-start | bytes 2097152 | tf_op jit(solution)/shard_map/psum | solution.py:27
  124.7 9.7 %copy-start.2 = (bf16[1792,512]{1,0:T(8,128)(2,1)S(1)}, bf16[1792,512]{1,0:T(8,128)(2,1)}, u32[]{:S(2)}) copy-start(bf16[1792,512]{1,0:T(8,128)(2,1)} %all-reduce.5.cloned.1.call-done) | copy-start | bytes 5505028
  134.1 358.0 %all-reduce.9.cloned.1.call-start = ((), (), s32[]{:S(2)}) async-start(), calls=%async_computation.3 | async-start | bytes 8388608 | tf_op jit(solution)/shard_map/psum | solution.py:34
  321.4 6.1 %copy-start.1 = (f32[512,1792]{0,1:T(8,128)S(1)}, f32[512,1792]{0,1:T(8,128)}, u32[]{:S(2)}) copy-start(f32[512,1792]{0,1:T(8,128)} %fusion.1) | copy-start | bytes 11010052
  326.5 11.8 %slice-start = ((s8[7340032]{0:T(1024)(128)(4,1)}), s8[4194304]{0:T(1024)(128)(4,1)S(1)}, s32[]{:S(2)}) async-start(s8[7340032]{0:T(1024)(128)(4,1)} %bitcast.66), calls=%async_computation.4 | async-start | bytes 8388608
  330.7 7.6 %slice-start.1 = ((s8[7340032]{0:T(1024)(128)(4,1)}), s8[3145728]{0:T(1024)(128)(4,1)S(1)}, s32[]{:S(2)}) async-start(s8[7340032]{0:T(1024)(128)(4,1)} %bitcast.66), calls=%async_computation.5 | async-start | bytes 6291456
  331.7 17.9 %copy-start.3 = (bf16[128,1792]{1,0:T(8,128)(2,1)}, bf16[128,1792]{1,0:T(8,128)(2,1)S(1)}, u32[]{:S(2)}) copy-start(bf16[128,1792]{1,0:T(8,128)(2,1)S(1)} %get-tuple-element.33) | copy-start | bytes 1376260
  337.5 0.8 copy-start.5
  492.1 3.4 copy-start
  495.6 1.0 copy-start.4
  495.6 1.2 copy-start.6
Sparse Core Ops, SparseCore 0:
  10.4 37.8 all-gather.1
  61.5 63.1 all-reduce.4
  134.3 52.4 all-reduce.6
  349.7 142.3 all-reduce.8
where the time goes:
time: 534 us; the launch traced here: 526 us
  waiting for transfers between devices  295 us (55%)
  other arithmetic  128 us (24%)
  matrix products  72.8 us (14%)
  between operations  17 us (3%)
  local copies, waits for them, and re-layouts  13.1 us (2%)
    psum x1, waiting for transfers between devices, per_device(): right_mean = lax.psum(partial_right, ('rep', 'rows')) / groups  143 us
    another operation x14, other arithmetic, per_device(): chol = jnp.linalg.cholesky(gram)  79 us
    psum x1, waiting for transfers between devices, per_device(): lax.psum(left_local.astype(jnp.bfloat16), 'rep').astype(jnp.float32)  63.3 us
    psum x1, waiting for transfers between devices, per_device(): lax.psum(jnp.dot(left_mean.T, left_mean, precision=lax.Precision.HIGHEST)...  50 us
    another operation x3, other arithmetic, per_device(): jax.scipy.linalg.solve_triangular(chol, left_mean.T, lower=True)  39.4 us
    all_gather x1, waiting for transfers between devices, per_device(): lax.all_gather(right_factor.astype(jnp.bfloat16), 'rows', axis=0, tiled=T...  39 us
    another operation x7, matrix products, per_device(): jax.scipy.linalg.solve_triangular(chol, left_mean.T, lower=True)  16 us
    dot_general x1, matrix products, per_device(): jnp.dot(combined_half, lax.all_gather(right_factor.astype(jnp.bfloat16),...  13.1 us
  transfers between devices with their start and end apart: 4, of which 4 were waited for; matrix products, arithmetic and copies ran while one was open for 0% of the time, Pallas kernels for 0%

commit v1 on v0

--- a/solution.py
+++ b/solution.py
@@ -1,3 +1,4 @@
+import functools
 import jax
 import jax.numpy as jnp
 from jax import lax
@@ -8,6 +9,13 @@
 momentum_keep = 0.05
 learn_rate = 0.5
 tiny = 1e-06
+
+
+def try_all_ranges(x_part, link_axis, mesh_ax):
+    return lax.psum(lax.psum(x_part, link_axis), mesh_ax)
+
+
+end_frames = functools.partial(try_all_ranges, link_axis="rows", mesh_ax="rep")
 
 
 def per_device(weights, momentum, gradient, right_factor):
@@ -31,7 +39,7 @@
     partial_right = jnp.einsum(
         "ij,ik->jk", combined_half, left_half, preferred_element_type=jnp.float32
     )
-    right_mean = lax.psum(partial_right, ("rep", "rows")) / groups
+    right_mean = end_frames(partial_right) / groups
     normed = right_mean / jnp.sqrt(jnp.mean(right_mean * right_mean, axis=0) + tiny)
     feedback = jnp.dot(
         left_half, right_mean.astype(jnp.bfloat16).T, preferred_element_type=jnp.float32

time: 534 us -> 594 us (1.11)
  waiting for transfers between devices: 295 us -> 355 us
    psum x1 -> x2, waiting for transfers between devices: 143 us -> 202 us  [try_all_ranges(): return lax.psum(lax.psum(x_part, link_axis), mesh_ax)]
  transfers between devices with their start and end apart: 4 -> 5, of which waited for: 4 -> 5; matrix products, arithmetic and copies ran while one was open for 0% -> 0% of each run, Pallas kernels for 0% -> 0%
where the time goes in v1:
time: 594 us; the launch traced here: 586 us
  waiting for transfers between devices  355 us (60%)
  other arithmetic  128 us (22%)
  matrix products  72.8 us (12%)
  between operations  17 us (3%)
  local copies, waits for them, and re-layouts  13.2 us (2%)
    psum x2, waiting for transfers between devices, try_all_ranges(): return lax.psum(lax.psum(x_part, link_axis), mesh_ax)  202 us
    another operation x14, other arithmetic, per_device(): chol = jnp.linalg.cholesky(gram)  79 us
    psum x1, waiting for transfers between devices, per_device(): lax.psum(left_local.astype(jnp.bfloat16), 'rep').astype(jnp.float32)  63.3 us
    psum x1, waiting for transfers between devices, per_device(): lax.psum(jnp.dot(left_mean.T, left_mean, precision=lax.Precision.HIGHEST)...  50 us
    another operation x3, other arithmetic, per_device(): jax.scipy.linalg.solve_triangular(chol, left_mean.T, lower=True)  39.4 us
    all_gather x1, waiting for transfers between devices, per_device(): lax.all_gather(right_factor.astype(jnp.bfloat16), 'rows', axis=0, tiled=T...  39 us
    another operation x7, matrix products, per_device(): jax.scipy.linalg.solve_triangular(chol, left_mean.T, lower=True)  16 us
    dot_general x1, matrix products, per_device(): jnp.dot(combined_half, lax.all_gather(right_factor.astype(jnp.bfloat16),...  13.1 us
  transfers between devices with their start and end apart: 5, of which 5 were waited for; matrix products, arithmetic and copies ran while one was open for 0% of the time, Pallas kernels for 0%

profile of v1, /device:TPU:0, one launch (start us, length us, event | category | flops | bytes accessed | tf_op | source)
XLA Modules:
  0.0 585.9 jit_solution(6376913870071803371)
XLA Ops:
  9.4 39.0 %all-gather.2.cloned.1.call-done = bf16[2048,512]{1,0:T(8,128)(2,1)} async-done(((bf16[512,512]{1,0:T(8,128)(2,1)}), bf16[2048,512]{1,0:T(8,128)(2,1)}) %all-gather.2.cloned.1.call-update) | async-done | bytes 2097168 | tf_op jit(solution)/shard_map/all_gather | solution.py:30
  48.3 13.1 %convolution_convert_fusion = bf16[1792,512]{1,0:T(8,128)(2,1)} fusion(bf16[2048,512]{1,0:T(8,128)(2,1)} %all-gather.2.cloned.1.call-done, f32[1,1792,2048]{2,1,0:T(8,128)} %param.5, bf16[1,1792,2048]{2,1,0:T(8,128)(2,1)} %param.6), kind=kOutput, calls=%fused_computation.13 | convolution fusion | flops 3770023936 | bytes 25952256 | tf_op jit(solution)/shard_map/dot_general | solution.py:28
  61.5 63.3 %all-reduce.6.cloned.1.call-done = bf16[1792,512]{1,0:T(8,128)(2,1)} async-done(((bf16[1792,512]{1,0:T(8,128)(2,1)}), bf16[1792,512]{1,0:T(8,128)(2,1)}) %all-reduce.6.cloned.1.call-update) | async-done | bytes 1835024 | tf_op jit(solution)/shard_map/psum | solution.py:34
  124.7 9.4 %fusion.2 = f32[512,512]{0,1:T(8,128)} fusion(bf16[1792,512]{1,0:T(8,128)(2,1)} %all-reduce.6.cloned.1.call-done), kind=kOutput, calls=%fused_computation.12 | convolution fusion | flops 5638979584 | bytes 2883584 | tf_op jit(solution)/shard_map/dot_general | solution.py:35
  134.4 2.4 fusion.1
  136.8 50.0 %all-reduce.8.cloned.1.call-done = f32[512,512]{0,1:T(8,128)} async-done(((f32[512,512]{0,1:T(8,128)}), f32[512,512]{0,1:T(8,128)}) %all-reduce.8.cloned.1.call-update) | async-done | bytes 1048592 | tf_op jit(solution)/shard_map/psum | solution.py:35
  189.8 11.7 %cholesky.104 = f32[128,128]{1,0:T(8,128)S(1)} custom-call(f32[128,128]{1,0:T(8,128)S(1)} %cholesky.266), custom_call_target="Cholesky" | custom-call | tf_op jit(solution)/shard_map/jit(cholesky)/cholesky | solution.py:36
  201.5 9.8 %custom-call.31 = f32[1,128,128]{1,2,0:T(8,128)S(1)} custom-call(f32[1,128,128]{2,1,0:T(8,128)S(1)} %get-tuple-element.30), custom_call_target="InvertDiagBlocksLowerTriangular" | custom-call | tf_op jit(solution)/shard_map/jit(cholesky)/cholesky | solution.py:36
  212.2 11.7 %cholesky.217 = f32[128,128]{1,0:T(8,128)S(1)} custom-call(f32[128,128]{1,0:T(8,128)S(1)} %cholesky.270), custom_call_target="Cholesky" | custom-call | tf_op jit(solution)/shard_map/jit(cholesky)/cholesky | solution.py:36
  223.9 10.2 %custom-call.32 = f32[1,128,128]{1,2,0:T(8,128)S(1)} custom-call(f32[1,128,128]{2,1,0:T(8,128)S(1)} %get-tuple-element.27), custom_call_target="InvertDiagBlocksLowerTriangular" | custom-call | tf_op jit(solution)/shard_map/jit(cholesky)/cholesky | solution.py:36
  234.8 11.7 %cholesky.238 = f32[128,128]{1,0:T(8,128)S(1)} custom-call(f32[128,128]{1,0:T(8,128)S(1)} %cholesky.275), custom_call_target="Cholesky" | custom-call | tf_op jit(solution)/shard_map/jit(cholesky)/cholesky | solution.py:36
  247.3 9.8 %custom-call.33 = f32[1,128,128]{1,2,0:T(8,128)S(1)} custom-call(f32[1,128,128]{2,1,0:T(8,128)S(1)} %get-tuple-element.24), custom_call_target="InvertDiagBlocksLowerTriangular" | custom-call | tf_op jit(solution)/shard_map/jit(cholesky)/cholesky | solution.py:36
  257.7 11.9 %cholesky.255 = f32[128,128]{1,0:T(8,128)S(1)} custom-call(f32[128,128]{1,0:T(8,128)S(1)} %convolution_subtract_fusion.4), custom_call_target="Cholesky" | custom-call | tf_op jit(solution)/shard_map/jit(cholesky)/cholesky | solution.py:36
  273.6 8.5 %while.1 = (s32[]{:T(128)}, f32[512,512]{1,0:T(8,128)S(1)}, s32[4,2]{0,1:T(2,128)S(1)}, f32[4,128,128]{2,1,0:T(8,128)S(1)}, s32[]{:T(128)}) while((s32[]{:T(128)}, f32[512,512]{1,0:T(8,128)S(1)}, s32[4,2]{0,1:T(2,128)S(1)}, f32[4,128,128]{2,1,0:T(8,128)S(1)}, s32[]{:T(128)}) %tuple.34), condition=%wide.while_cond, body=%wide.while_body.sunk | while | flops 2 | bytes 131181 | solution.py:37
  282.1 39.3 %custom-call.34 = f32[4,128,128]{1,2,0:T(8,128)S(1)} custom-call(f32[4,128,128]{2,1,0:T(8,128)S(1)} %get-tuple-element.10), custom_call_target="InvertDiagBlocksLowerTriangular" | custom-call | tf_op jit(solution)/shard_map/jit(_solve_triangular)/triangular_solve | solution.py:37
  323.7 2.8 convolution_subtract_fusion.1
  327.5 3.2 convolution_subtract_fusion
  331.7 4.7 fusion.9
  338.4 11.3 %fusion.41 = f32[2048,512]{1,0:T(8,128)} fusion(f32[1,1792,2048]{2,1,0:T(8,128)} %param.5, bf16[1,1792,2048]{2,1,0:T(8,128)(2,1)S(1)} %bitcast.67, bf16[128,1792]{1,0:T(8,128)(2,1)S(1)} %convolution_convert_fusion.1, bf16[128,1792]{1,0:T(8,128)(2,1)S(1)} %get-tuple-element.33, bf16[128,1792]{1,0:T(8,128)(2,1)S(1)} %get-tuple-element.35, ...), kind=kOutput, calls=%fused_computation.86 | convolution fusion | flops 3776446464 | bytes 28049408 | tf_op jit(solution)/shard_map/ij,ik->jk/dot_general | solution.py:39
  349.7 103.7 %all-reduce.10.cloned.1.call-done = f32[2048,512]{1,0:T(8,128)} async-done(((f32[2048,512]{1,0:T(8,128)}), f32[2048,512]{1,0:T(8,128)}) %all-reduce.10.cloned.1.call-update) | async-done | bytes 4194320 | tf_op jit(solution)/shard_map/psum | solution.py:15
  453.5 98.7 %all-reduce.12.cloned.1.call-done = f32[2048,512]{1,0:T(8,128)} async-done(((f32[2048,512]{1,0:T(8,128)}), f32[2048,512]{1,0:T(8,128)}) %all-reduce.12.cloned.1.call-update) | async-done | bytes 4194320 | tf_op jit(solution)/shard_map/psum | solution.py:15
  552.2 2.9 multiply_reduce_fusion
  556.8 8.2 %subtract_convert_fusion = bf16[1792,2048]{1,0:T(8,128)(2,1)} fusion(bf16[1792,2048]{1,0:T(8,128)(2,1)} %param.4, f32[2048,512]{1,0:T(8,128)S(1)} %multiply_divide_fusion, bf16[128,1792]{1,0:T(8,128)(2,1)S(1)} %copy-done.6, bf16[128,1792]{1,0:T(8,128)(2,1)S(1)} %copy-done.4, bf16[128,1792]{1,0:T(8,128)(2,1)S(1)} %get-tuple-element.35, ...), kind=kOutput, calls=%fused_computation.5 | convolution fusion | flops 3781165056 | bytes 20709376 | tf_op jit(solution)/shard_map/dot_general | solution.py:47
  566.0 13.0 %fusion = f32[1,1792,2048]{2,1,0:T(8,128)} fusion(f32[1,1792,2048]{2,1,0:T(8,128)} %param.5, bf16[1,1792,2048]{2,1,0:T(8,128)(2,1)} %param.6, f32[2048,512]{1,0:T(8,128)S(1)} %copy-done, bf16[128,1792]{1,0:T(8,128)(2,1)} %copy-done.5, bf16[128,1792]{1,0:T(8,128)(2,1)} %copy-done.3, bf16[128,1792]{1,0:T(8,128)(2,1)S(1)} %get-tuple-element.35, ...), kind=kOutput, calls=%fused_computation.4 | convolution fusion | flops 3782213632 | bytes 42729472 | tf_op jit(solution)/shard_map/dot_general | solution.py:44
  (72 shorter events, 27.3 us)
Async XLA Ops:
  7.2 41.2 %all-gather.2.cloned.1.call-start = ((), (), s32[]{:S(2)}) async-start(), calls=%async_computation | async-start | bytes 2621440 | tf_op jit(solution)/shard_map/all_gather | solution.py:30
  9.3 115.4 %all-reduce.6.cloned.1.call-start = ((), (), s32[]{:S(2)}) async-start(), calls=%async_computation.1 | async-start | bytes 3670016 | tf_op jit(solution)/shard_map/psum | solution.py:34
  61.4 125.4 %all-reduce.8.cloned.1.call-start = ((), (), s32[]{:S(2)}) async-start(), calls=%async_computation.2 | async-start | bytes 2097152 | tf_op jit(solution)/shard_map/psum | solution.py:35
  124.7 9.7 %copy-start.2 = (bf16[1792,512]{1,0:T(8,128)(2,1)S(1)}, bf16[1792,512]{1,0:T(8,128)(2,1)}, u32[]{:S(2)}) copy-start(bf16[1792,512]{1,0:T(8,128)(2,1)} %all-reduce.6.cloned.1.call-done) | copy-start | bytes 5505028
  134.1 319.3 %all-reduce.10.cloned.1.call-start = ((), (), s32[]{:S(2)}) async-start(), calls=%async_computation.3 | async-start | bytes 8388608 | tf_op jit(solution)/shard_map/psum | solution.py:15
  321.4 6.1 %copy-start.1 = (f32[512,1792]{0,1:T(8,128)S(1)}, f32[512,1792]{0,1:T(8,128)}, u32[]{:S(2)}) copy-start(f32[512,1792]{0,1:T(8,128)} %fusion.1) | copy-start | bytes 11010052
  326.5 11.8 %slice-start = ((s8[7340032]{0:T(1024)(128)(4,1)}), s8[4194304]{0:T(1024)(128)(4,1)S(1)}, s32[]{:S(2)}) async-start(s8[7340032]{0:T(1024)(128)(4,1)} %bitcast.66), calls=%async_computation.5 | async-start | bytes 8388608
  330.7 7.7 %slice-start.1 = ((s8[7340032]{0:T(1024)(128)(4,1)}), s8[3145728]{0:T(1024)(128)(4,1)S(1)}, s32[]{:S(2)}) async-start(s8[7340032]{0:T(1024)(128)(4,1)} %bitcast.66), calls=%async_computation.6 | async-start | bytes 6291456
  331.7 18.0 %copy-start.3 = (bf16[128,1792]{1,0:T(8,128)(2,1)}, bf16[128,1792]{1,0:T(8,128)(2,1)S(1)}, u32[]{:S(2)}) copy-start(bf16[128,1792]{1,0:T(8,128)(2,1)S(1)} %get-tuple-element.33) | copy-start | bytes 1376260
  337.5 0.8 copy-start.5
  349.7 202.5 %all-reduce.12.cloned.1.call-start = ((), (), s32[]{:S(2)}) async-start(), calls=%async_computation.4 | async-start | bytes 8388608 | tf_op jit(solution)/shard_map/psum | solution.py:15
  552.2 3.4 copy-start
  555.6 1.0 copy-start.4
  555.6 1.2 copy-start.6
Sparse Core Ops, SparseCore 0:
  10.4 37.8 all-gather.1
  61.5 63.1 all-reduce.5
  134.3 52.4 all-reduce.7
  349.8 103.6 all-reduce.9
  455.6 96.4 all-reduce.11
